TPU v7x, 512 devices: a whole 4x8x8 slice. The times are simulated.
512 devices in a mesh: dp: 8 (over z), expert: 64 (over y, x, core).
Axes of the slice: x: 4, y: 8, z: 8, core: 2. Of those that a mesh axis runs over, the one named last changes fastest.
Arguments:
- tokens: bfloat16 [65536, 3584], P(('dp', 'expert')), may hold values from -6 to 6
- cotangent: bfloat16 [65536, 3584], P(('dp', 'expert')), may hold values from -6 to 6
- route_ids: int32 [65536, 8], P(('dp', 'expert')), may hold values from 0 to 255, as said below
- route_gates: float32 [65536, 8], P(('dp', 'expert')), may hold values from 0.1 to 1
- gate_w: bfloat16 [3584, 8192], P('dp', 'expert'), may hold values from -0.09375 to 0.09375
- up_w: bfloat16 [3584, 8192], P('dp', 'expert'), may hold values from -0.09375 to 0.09375
- down_w: bfloat16 [3584, 8192], P('dp', 'expert'), may hold values from -0.1875 to 0.1875
Outputs:
- moe_out: bfloat16 [65536, 3584], P(('dp', 'expert'))
- d_tokens: bfloat16 [65536, 3584], P(('dp', 'expert'))
- d_gates: float32 [65536, 8], P(('dp', 'expert'))
- d_gate_w: bfloat16 [3584, 8192], P('dp', 'expert')
- d_up_w: bfloat16 [3584, 8192], P('dp', 'expert')
- d_down_w: bfloat16 [3584, 8192], P('dp', 'expert')
Inputs may be any that keep to these rules, and one draw needn't show every extreme that they name: `route_ids`: each token names 8 different experts; the experts in flight are 0 to 7. Among the tokens of one device (aligned blocks of 128 tokens) each expert in flight is named by at most 6 tokens, and in every draw one expert in flight is named by exactly 6 tokens in every block.
All inputs are finite; a program needn't handle non-finite values.
Results may differ from a plain program's by a relative error of at most 0.017.
Values may be sent and summed in bfloat16 or wider, within the bound.
A program may use at most 64 MiB of HBM per device.

v0:
```python
import jax
import jax.numpy as jnp
from jax import lax
from jax.sharding import Mesh, PartitionSpec as P

SLICES = 8
CAP = 6
PAD = 8
BF = jnp.bfloat16
F32 = jnp.float32
CONTRACT_COLS = (((1,), (1,)), ((), ()))
CONTRACT_ROWS = (((0,), (0,)), ((), ()))


def dot(a, b, dims=(((1,), (0,)), ((), ()))):
    return lax.dot_general(a, b, dims, preferred_element_type=F32)


def routing(route_ids, route_gates, groups):
    tok_rows = route_ids.shape[0]
    experts = jnp.arange(groups, dtype=jnp.int32)
    match = route_ids[:, :, None] == experts[None, None, :]
    member = jnp.sum(match.astype(F32), axis=1)
    gate = jnp.sum(jnp.where(match, route_gates[:, :, None], 0.0), axis=1)
    row = lax.broadcasted_iota(jnp.int32, (tok_rows, tok_rows), 0)
    col = lax.broadcasted_iota(jnp.int32, (tok_rows, tok_rows), 1)
    before = (col < row).astype(BF)
    slot = dot(before, member.astype(BF))
    return (match, member, gate, slot)


def shards(tokens, cotangent, route_ids, route_gates, gate_w, up_w, down_w):
    groups = lax.axis_size("y")
    width = tokens.shape[1]
    tok_rows = tokens.shape[0]
    hid = gate_w.shape[1]
    match, member, gate, slot = routing(route_ids, route_gates, groups)
    wide = jnp.where(member > 0.5, slot, -1.0).T[:, None, :]
    sel = (wide == jnp.arange(PAD, dtype=F32)[None, :, None]).astype(F32)
    gates_t = gate.T[:, None, :]
    slot_gate = jnp.sum(sel * gates_t, axis=2)
    pick = sel.reshape(groups * PAD, tok_rows).astype(BF)
    token_slots = dot(pick, tokens).astype(BF)
    cot_slots = dot(pick, cotangent)
    scaled_slots = (slot_gate.reshape(groups * PAD, 1) * cot_slots).astype(BF)
    send = jnp.concatenate(
        [token_slots.reshape(groups, PAD, width), scaled_slots.reshape(groups, PAD, width)], axis=1
    )
    w_all = lax.all_gather(
        jnp.concatenate([gate_w, up_w, down_w], axis=1), "dp", axis=0, tiled=True
    )
    w_gate, w_up, w_down = (w_all[:, :hid], w_all[:, hid : 2 * hid], w_all[:, 2 * hid :])
    came = lax.all_to_all(send, "y", split_axis=0, concat_axis=0, tiled=True)
    rows = groups * CAP
    out_row = lax.broadcasted_iota(jnp.int32, (2 * rows, groups * 2 * PAD), 0)
    in_row = lax.broadcasted_iota(jnp.int32, (2 * rows, groups * 2 * PAD), 1)
    kind = (out_row >= rows).astype(jnp.int32)
    local = out_row - kind * rows
    wanted = local // CAP * (2 * PAD) + kind * PAD + local % CAP
    squeeze = (in_row == wanted).astype(BF)
    compact = dot(squeeze, came.reshape(groups * 2 * PAD, width)).astype(BF)
    both = lax.all_gather(compact, ("x", "c"), axis=0, tiled=False)
    n_slices = both.shape[0]
    token_rows = both[:, :rows].reshape(n_slices * rows, width)
    scaled_rows = both[:, rows:].reshape(n_slices * rows, width)
    gate_pre = dot(token_rows, w_gate)
    up_pre = dot(token_rows, w_up)
    sig = jax.nn.sigmoid(gate_pre)
    active = gate_pre * sig
    hidden = (active * up_pre).astype(BF)
    d_hidden = dot(scaled_rows, w_down)
    d_gate_pre = (d_hidden * up_pre * sig * (1.0 + gate_pre * (1.0 - sig))).astype(BF)
    d_up_pre = (d_hidden * active).astype(BF)
    out_part = dot(hidden, w_down, CONTRACT_COLS).astype(BF)
    dx_part = (dot(d_gate_pre, w_gate, CONTRACT_COLS) + dot(d_up_pre, w_up, CONTRACT_COLS)).astype(
        BF
    )
    parts = jnp.concatenate(
        [out_part.reshape(n_slices, rows, width), dx_part.reshape(n_slices, rows, width)], axis=1
    ).reshape(n_slices * 2 * rows, width)
    summed = lax.psum_scatter(parts, ("x", "c"), scatter_dimension=0, tiled=True)
    grads = jnp.concatenate(
        [
            dot(token_rows, d_gate_pre, CONTRACT_ROWS),
            dot(token_rows, d_up_pre, CONTRACT_ROWS),
            dot(scaled_rows, hidden, CONTRACT_ROWS),
        ],
        axis=1,
    ).astype(BF)
    grads = lax.psum_scatter(grads, "dp", scatter_dimension=0, tiled=True)
    back = dot(squeeze, summed, CONTRACT_ROWS).astype(BF).reshape(groups, 2 * PAD, width)
    back = lax.all_to_all(back, "y", split_axis=0, concat_axis=0, tiled=True)
    back = back.reshape(groups * 2 * PAD, width)
    zero = jnp.zeros_like(sel)
    member_out = jnp.concatenate([sel, zero], axis=1).reshape(groups * 2 * PAD, tok_rows)
    member_dx = jnp.concatenate([zero, sel], axis=1).reshape(groups * 2 * PAD, tok_rows)
    weight = jnp.concatenate([sel * gates_t, zero], axis=1).reshape(groups * 2 * PAD, tok_rows)
    high = weight.astype(BF)
    low = (weight - high.astype(F32)).astype(BF)
    moe_out = (dot(high, back, CONTRACT_ROWS) + dot(low, back, CONTRACT_ROWS)).astype(BF)
    d_tokens = dot(member_dx.astype(BF), back, CONTRACT_ROWS).astype(BF)
    inner = dot(back, cotangent, CONTRACT_COLS) * member_out
    by_expert = jnp.sum(inner.reshape(groups, 2 * PAD, tok_rows), axis=1).T
    d_gates = jnp.sum(jnp.where(match, by_expert[:, None, :], 0.0), axis=2)
    return (
        moe_out,
        d_tokens,
        d_gates,
        grads[:, :hid],
        grads[:, hid : 2 * hid],
        grads[:, 2 * hid :],
    )


def solution(mesh):
    dp, owners = mesh.devices.shape
    y = owners // SLICES
    grid = Mesh(mesh.devices.reshape(dp, y, SLICES // 2, 2), ("dp", "y", "x", "c"))
    rows = P(("dp", "y", "x", "c"), None)
    cols = P("dp", ("y", "x", "c"))
    return jax.shard_map(
        shards,
        mesh=grid,
        in_specs=(rows, rows, rows, rows, cols, cols, cols),
        out_specs=(rows, rows, rows, cols, cols, cols),
        check_vma=False,
    )
```

profile of v0, /device:TPU:2, one launch (start us, length us, event | category | flops | bytes accessed | tf_op | source)
XLA Modules:
  0.0 255.6 jit_solution(2671036714309216586)
XLA Ops:
  7.2 0.0 copy-start
  7.2 0.8 convert_reduce_fusion
  8.0 0.1 convolution_select_fusion
  8.1 0.1 fusion.22
  8.2 0.1 mul.76
  8.3 0.1 eq.53
  8.4 1.5 fusion.6
  9.9 0.3 fusion.5
  10.3 0.0 copy-start.7
  10.3 1.0 pad_maximum_fusion.2
  11.3 7.1 %all-to-all-start = ((bf16[8,16,3584]{2,1,0:T(8,128)(2,1)}), bf16[8,16,3584]{2,1,0:T(8,128)(2,1)S(1)}, u32[]{:S(2)}, u32[]{:S(2)}) async-start(bf16[8,16,3584]{2,1,0:T(8,128)(2,1)} %pad_maximum_fusion.2), calls=%async_computation | async-start | bytes 1835008 | tf_op jit(solution)/shard_map/all_to_all | solution.py:53
  18.4 0.0 all-gather.6.cloned.1.call-start
  18.5 25.8 %all-to-all-done = bf16[8,16,3584]{2,1,0:T(8,128)(2,1)S(1)} async-done(((bf16[8,16,3584]{2,1,0:T(8,128)(2,1)}), bf16[8,16,3584]{2,1,0:T(8,128)(2,1)S(1)}, u32[]{:S(2)}, u32[]{:S(2)}) %all-to-all-start) | async-done | bytes 917536 | tf_op jit(solution)/shard_map/all_to_all | solution.py:53
  44.3 1.3 convolution_convert_fusion.5
  45.6 0.0 all-gather.6.cloned.1.call-update
  45.6 0.0 all-gather.4.cloned.1.call-start
  45.7 0.8 pad_maximum_fusion.3
  46.5 0.0 all-gather.4.cloned.1.call-update
  46.5 0.0 reduce-scatter.5.cloned.1.call-start
  46.5 40.6 %all-gather.6.cloned.1.call-done = bf16[768,3584]{1,0:T(8,128)(2,1)} async-done(((bf16[96,3584]{1,0:T(8,128)(2,1)}), bf16[768,3584]{1,0:T(8,128)(2,1)}) %all-gather.6.cloned.1.call-update) | async-done | bytes 5505040 | tf_op jit(solution)/shard_map/all_gather | solution.py:62
  87.2 5.5 %fusion.33 = (bf16[8,48,3584]{2,1,0:T(8,128)(2,1)}, bf16[8,48,3584]{2,1,0:T(8,128)(2,1)}) fusion(bf16[8,96,3584]{2,1,0:T(8,128)(2,1)} %bitcast.70), kind=kLoop, calls=%fused_computation.75 | loop fusion | bytes 11010048 | tf_op jit(solution)/shard_map/slice | solution.py:65
  92.6 44.5 %all-gather.4.cloned.1.call-done = bf16[3584,384]{1,0:T(8,128)(2,1)} async-done(((bf16[448,384]{1,0:T(8,128)(2,1)}), bf16[3584,384]{1,0:T(8,128)(2,1)}) %all-gather.4.cloned.1.call-update) | async-done | bytes 2752528 | tf_op jit(solution)/shard_map/all_gather | solution.py:49
  137.1 3.0 %fusion.15 = f32[384,128]{1,0:T(8,128)S(1)} fusion(bf16[384,3584]{1,0:T(8,128)(2,1)} %bitcast.60, bf16[3584,384]{1,0:T(8,128)(2,1)} %all-gather.4.cloned.1.call-done), kind=kOutput, calls=%fused_computation.32 | convolution fusion | flops 352321536 | bytes 3866624 | tf_op jit(solution)/shard_map/dot_general | solution.py:16
  140.2 2.2 fusion.7
  142.4 0.9 multiply_convert_fusion.2
  143.3 0.9 fusion.13
  144.2 0.9 convolution_convert_fusion
  145.0 0.9 fusion
  145.9 2.8 %pad_maximum_fusion = bf16[8,96,3584]{2,1,0:T(8,128)(2,1)} fusion(bf16[8,48,3584]{2,1,0:T(8,128)(2,1)S(1)} %bitcast.69, bf16[8,48,3584]{2,1,0:T(8,128)(2,1)S(1)} %bitcast.68), kind=kLoop, calls=%fused_computation.3 | loop fusion | flops 11010048 | bytes 11010048 | tf_op jit(solution)/shard_map/concatenate | solution.py:78
  148.7 0.0 reduce-scatter.5.cloned.1.call-update
  148.7 0.0 reduce-scatter.7.cloned.1.call-start
  148.8 2.6 %convolution_convert_fusion.1 = bf16[3584,128]{0,1:T(8,128)(2,1)S(1)} fusion(bf16[384,3584]{1,0:T(8,128)(2,1)} %bitcast.66, bf16[384,128]{1,0:T(8,128)(2,1)S(1)} %get-tuple-element.28), kind=kOutput, calls=%fused_computation.10 | convolution fusion | flops 352780288 | bytes 3768320 | tf_op jit(solution)/shard_map/dot_general | solution.py:16
  151.4 0.7 convolution_convert_fusion.2
  152.1 0.7 convolution_convert_fusion.3
  152.8 1.8 pad_maximum_fusion.1
  154.6 4.5 %copy.27 = bf16[3584,384]{1,0:T(8,128)(2,1)} copy(bf16[3584,384]{0,1:T(8,128)(2,1)} %pad_maximum_fusion.1) | data formatting | bytes 5505024
  159.1 0.0 reduce-scatter.7.cloned.1.call-update
  159.2 0.0 copy-start.8
  159.2 30.2 %reduce-scatter.5.cloned.1.call-done = bf16[96,3584]{1,0:T(8,128)(2,1)} async-done(((bf16[768,3584]{1,0:T(8,128)(2,1)}), bf16[96,3584]{1,0:T(8,128)(2,1)}) %reduce-scatter.5.cloned.1.call-update) | async-done | bytes 688144 | tf_op jit(solution)/shard_map/reduce_scatter | solution.py:81
  189.3 2.6 %convolution_convert_fusion.4 = bf16[128,3584]{1,0:T(8,128)(2,1)} fusion(bf16[96,3584]{1,0:T(8,128)(2,1)} %reduce-scatter.5.cloned.1.call-done, s32[96]{0:T(128)S(1)} %broadcast_remainder_fusion, s32[96]{0:T(128)S(1)} %get-tuple-element.42, s32[96]{0:T(128)S(1)} %get-tuple-element.40, s32[96]{0:T(128)S(1)} %get-tuple-element.43, ...), kind=kOutput, calls=%fused_computation.13 | convolution fusion | flops 88612864 | bytes 1607744 | tf_op jit(solution)/shard_map/dot_general | solution.py:16
  191.9 6.8 %all-to-all-start.1 = ((bf16[8,16,3584]{2,1,0:T(8,128)(2,1)}), bf16[8,16,3584]{2,1,0:T(8,128)(2,1)S(1)}, u32[]{:S(2)}, u32[]{:S(2)}) async-start(bf16[8,16,3584]{2,1,0:T(8,128)(2,1)} %bitcast.12), calls=%async_computation.2 | async-start | bytes 1835008 | tf_op jit(solution)/shard_map/all_to_all | solution.py:92
  198.8 44.4 %reduce-scatter.7.cloned.1.call-done = bf16[448,384]{1,0:T(8,128)(2,1)} async-done(((bf16[3584,384]{1,0:T(8,128)(2,1)}), bf16[448,384]{1,0:T(8,128)(2,1)}) %reduce-scatter.7.cloned.1.call-update) | async-done | bytes 344080
  243.2 1.7 fusion.34
  245.0 0.4 bitcast_reduce_fusion
  245.4 0.6 select_reduce_fusion
  246.0 0.4 convolution_bitcast_fusion.1
  246.4 1.4 fusion.2
  247.8 1.3 fusion.3
  (23 shorter events, 0.1 us)
Async XLA Ops:
  7.2 2.8 %copy-start = (bf16[128,3584]{1,0:T(8,128)(2,1)S(1)}, bf16[128,3584]{1,0:T(8,128)(2,1)}, u32[]{:S(2)}) copy-start(bf16[128,3584]{1,0:T(8,128)(2,1)} %param.8) | copy-start | bytes 2752516
  10.3 35.4 %copy-start.5 = (bf16[448,128]{1,0:T(8,128)(2,1)S(1)}, bf16[448,128]{1,0:T(8,128)(2,1)}, u32[]{:S(2)}) copy-start(bf16[448,128]{1,0:T(8,128)(2,1)} %param.13) | copy-start | bytes 344068
  10.3 35.4 %copy-start.6 = (bf16[448,128]{1,0:T(8,128)(2,1)S(1)}, bf16[448,128]{1,0:T(8,128)(2,1)}, u32[]{:S(2)}) copy-start(bf16[448,128]{1,0:T(8,128)(2,1)} %param.12) | copy-start | bytes 344068
  10.3 35.4 %copy-start.7 = (bf16[448,128]{1,0:T(8,128)(2,1)S(1)}, bf16[448,128]{1,0:T(8,128)(2,1)}, u32[]{:S(2)}) copy-start(bf16[448,128]{1,0:T(8,128)(2,1)} %param.11) | copy-start | bytes 344068
  11.3 33.0 %all-to-all-start = ((bf16[8,16,3584]{2,1,0:T(8,128)(2,1)}), bf16[8,16,3584]{2,1,0:T(8,128)(2,1)S(1)}, u32[]{:S(2)}, u32[]{:S(2)}) async-start(bf16[8,16,3584]{2,1,0:T(8,128)(2,1)} %pad_maximum_fusion.2), calls=%async_computation | async-start | bytes 1835008 | tf_op jit(solution)/shard_map/all_to_all | solution.py:53
  18.4 68.8 %all-gather.6.cloned.1.call-start = ((), (), s32[]{:S(2)}) async-start(), calls=%async_computation.6 | async-start | bytes 6193152 | tf_op jit(solution)/shard_map/all_gather | solution.py:62
  45.6 91.5 %all-gather.4.cloned.1.call-start = ((), (), s32[]{:S(2)}) async-start(), calls=%async_computation.4 | async-start | bytes 3096576 | tf_op jit(solution)/shard_map/all_gather | solution.py:49
  46.5 142.8 %reduce-scatter.5.cloned.1.call-start = ((), (), s32[]{:S(2)}) async-start(), calls=%async_computation.5 | async-start | bytes 6193152 | tf_op jit(solution)/shard_map/reduce_scatter | solution.py:81
  137.1 3.0 %copy-start.3 = (bf16[8,48,3584]{2,1,0:T(8,128)(2,1)S(1)}, bf16[8,48,3584]{2,1,0:T(8,128)(2,1)}, u32[]{:S(2)}) copy-start(bf16[8,48,3584]{2,1,0:T(8,128)(2,1)} %get-tuple-element.26) | copy-start | bytes 8257540
  137.1 5.3 %copy-start.4 = (bf16[3584,384]{1,0:T(8,128)(2,1)S(1)}, bf16[3584,384]{1,0:T(8,128)(2,1)}, u32[]{:S(2)}) copy-start(bf16[3584,384]{1,0:T(8,128)(2,1)} %all-gather.4.cloned.1.call-done) | copy-start | bytes 8257540
  140.2 2.2 copy-start.1
  148.7 94.5 %reduce-scatter.7.cloned.1.call-start = ((), (), s32[]{:S(2)}) async-start(), calls=%async_computation.7 | async-start | bytes 3096576
  148.8 2.6 %copy-start.2 = (bf16[8,48,3584]{2,1,0:T(8,128)(2,1)S(1)}, bf16[8,48,3584]{2,1,0:T(8,128)(2,1)}, u32[]{:S(2)}) copy-start(bf16[8,48,3584]{2,1,0:T(8,128)(2,1)} %get-tuple-element.27) | copy-start | bytes 8257540
  159.2 86.2 %copy-start.8 = (s32[128,8]{0,1:T(8,128)S(1)}, s32[128,8]{0,1:T(8,128)}, u32[]{:S(2)}) copy-start(s32[128,8]{0,1:T(8,128)} %param.9) | copy-start | bytes 12292
  191.9 53.0 %all-to-all-start.1 = ((bf16[8,16,3584]{2,1,0:T(8,128)(2,1)}), bf16[8,16,3584]{2,1,0:T(8,128)(2,1)S(1)}, u32[]{:S(2)}, u32[]{:S(2)}) async-start(bf16[8,16,3584]{2,1,0:T(8,128)(2,1)} %bitcast.12), calls=%async_computation.2 | async-start | bytes 1835008 | tf_op jit(solution)/shard_map/all_to_all | solution.py:92
Sparse Core Ops, SparseCore 0:
  45.7 41.3 all-gather.5
  89.8 47.2 all-gather.3
  148.8 40.4 reduce-scatter.4
  192.0 51.1 reduce-scatter.6
where the time goes:
time: 256 us
  waiting for transfers between devices  186 us (73%)
  matrix products  22.1 us (9%)
  starting transfers between devices  14.1 us (6%)
  between operations  14 us (5%)
  local copies, waits for them, and re-layouts  12 us (5%)
  other arithmetic  7.87 us (3%)
    unnamed x5, waiting for transfers between devices  44.5 us
    all_gather x1, waiting for transfers between devices, shards(): lax.all_gather(jnp.concatenate([gate_w, up_w, down_w], axis=1), 'dp', axi...  44.5 us
    all_gather x1, waiting for transfers between devices, shards(): both = lax.all_gather(compact, ('x', 'c'), axis=0, tiled=False)  40.6 us
    reduce_scatter x1, waiting for transfers between devices, shards(): lax.psum_scatter(parts, ('x', 'c'), scatter_dimension=0, tiled=True)  30.2 us
    all_to_all x1, waiting for transfers between devices, shards(): came = lax.all_to_all(send, 'y', split_axis=0, concat_axis=0, tiled=True)  25.8 us
    dot_general x18, matrix products, dot(): return lax.dot_general(a, b, dims, preferred_element_type=F32)  22.1 us
    all_to_all x1, starting transfers between devices, shards(): came = lax.all_to_all(send, 'y', split_axis=0, concat_axis=0, tiled=True)  7.09 us
    all_to_all x1, starting transfers between devices, shards(): back = lax.all_to_all(back, 'y', split_axis=0, concat_axis=0, tiled=True)  6.82 us
  transfers between devices with their start and end apart: 6, of which 5 were waited for; matrix products, arithmetic and copies ran while one was open for 8% of the time, Pallas kernels for 0%

commit v1 on v0

--- a/solution.py
+++ b/solution.py
@@ -46,8 +46,14 @@
     send = jnp.concatenate(
         [token_slots.reshape(groups, PAD, width), scaled_slots.reshape(groups, PAD, width)], axis=1
     )
-    w_all = lax.all_gather(
-        jnp.concatenate([gate_w, up_w, down_w], axis=1), "dp", axis=0, tiled=True
+    w_all = jnp.concatenate(
+        lax.all_to_all(
+            jnp.stack([jnp.concatenate([gate_w, up_w, down_w], axis=1)] * lax.axis_size("dp")),
+            "dp",
+            0,
+            0,
+        ),
+        axis=0,
     )
     w_gate, w_up, w_down = (w_all[:, :hid], w_all[:, hid : 2 * hid], w_all[:, 2 * hid :])
     came = lax.all_to_all(send, "y", split_axis=0, concat_axis=0, tiled=True)

time: 256 us -> 241 us (0.941)
  waiting for transfers between devices: 186 us -> 154 us
  starting transfers between devices: 14.1 us -> 24.4 us
  matrix products: 22.1 us -> 26.9 us
    all_gather x1 -> x0, waiting for transfers between devices: 44.5 us -> none  [shards(): lax.all_gather(jnp.concatenate([gate_w, up_w, down_w], axis=1), 'dp', axi...]
    all_to_all x0 -> x1, waiting for transfers between devices: none -> 30.7 us  [shards(): lax.all_to_all(jnp.stack([jnp.concatenate([gate_w, up_w, down_w], axis=1)...]
    all_gather x1, waiting for transfers between devices: 40.6 us -> 29.3 us  [shards(): both = lax.all_gather(compact, ('x', 'c'), axis=0, tiled=False)]
    all_to_all x0 -> x1, starting transfers between devices: none -> 10.3 us  [shards(): lax.all_to_all(jnp.stack([jnp.concatenate([gate_w, up_w, down_w], axis=1)...]
    reduce_scatter x1, waiting for transfers between devices: 30.2 us -> 22.9 us  [shards(): lax.psum_scatter(parts, ('x', 'c'), scatter_dimension=0, tiled=True)]
    dot_general x18, matrix products: 22.1 us -> 26.9 us  [dot(): return lax.dot_general(a, b, dims, preferred_element_type=F32)]
    unnamed x5 -> x4, waiting for transfers between devices: 44.5 us -> 44.9 us
  transfers between devices with their start and end apart: 6 -> 6, of which waited for: 5 -> 5; matrix products, arithmetic and copies ran while one was open for 8% -> 9% of each run, Pallas kernels for 0% -> 0%
where the time goes in v1:
time: 241 us; the launch traced here: 240 us
  waiting for transfers between devices  154 us (64%)
  matrix products  26.9 us (11%)
  starting transfers between devices  24.4 us (10%)
  between operations  14 us (6%)
  local copies, waits for them, and re-layouts  13.8 us (6%)
  other arithmetic  7.16 us (3%)
    unnamed x4, waiting for transfers between devices  44.9 us
    all_to_all x1, waiting for transfers between devices, shards(): lax.all_to_all(jnp.stack([jnp.concatenate([gate_w, up_w, down_w], axis=1)...  30.7 us
    all_gather x1, waiting for transfers between devices, shards(): both = lax.all_gather(compact, ('x', 'c'), axis=0, tiled=False)  29.3 us
    dot_general x18, matrix products, dot(): return lax.dot_general(a, b, dims, preferred_element_type=F32)  26.9 us
    all_to_all x1, waiting for transfers between devices, shards(): came = lax.all_to_all(send, 'y', split_axis=0, concat_axis=0, tiled=True)  25.8 us
    reduce_scatter x1, waiting for transfers between devices, shards(): lax.psum_scatter(parts, ('x', 'c'), scatter_dimension=0, tiled=True)  22.9 us
    all_to_all x1, starting transfers between devices, shards(): lax.all_to_all(jnp.stack([jnp.concatenate([gate_w, up_w, down_w], axis=1)...  10.3 us
    all_to_all x1, starting transfers between devices, shards(): came = lax.all_to_all(send, 'y', split_axis=0, concat_axis=0, tiled=True)  7.09 us
  transfers between devices with their start and end apart: 6, of which 5 were waited for; matrix products, arithmetic and copies ran while one was open for 9% of the time, Pallas kernels for 0%

profile of v1, /device:TPU:2, one launch (start us, length us, event | category | flops | bytes accessed | tf_op | source)
XLA Modules:
  0.0 239.8 jit_solution(6471828938322069583)
XLA Ops:
  7.2 0.0 copy-start
  7.2 0.8 convert_reduce_fusion
  8.0 0.1 convolution_select_fusion
  8.1 0.1 fusion.22
  8.2 0.1 mul.76
  8.3 0.1 eq.53
  8.4 1.5 fusion.6
  9.9 0.3 fusion.5
  10.3 0.0 copy-start.4
  10.3 0.0 copy-start.5
  10.3 0.0 copy-start.6
  10.3 1.0 pad_maximum_fusion.2
  11.3 7.1 %all-to-all-start = ((bf16[8,16,3584]{2,1,0:T(8,128)(2,1)}), bf16[8,16,3584]{2,1,0:T(8,128)(2,1)S(1)}, u32[]{:S(2)}, u32[]{:S(2)}) async-start(bf16[8,16,3584]{2,1,0:T(8,128)(2,1)} %pad_maximum_fusion.2), calls=%async_computation | async-start | bytes 1835008 | tf_op jit(solution)/shard_map/all_to_all | solution.py:59
  18.4 0.0 all-gather.3.cloned.1.call-start
  18.5 25.8 %all-to-all-done = bf16[8,16,3584]{2,1,0:T(8,128)(2,1)S(1)} async-done(((bf16[8,16,3584]{2,1,0:T(8,128)(2,1)}), bf16[8,16,3584]{2,1,0:T(8,128)(2,1)S(1)}, u32[]{:S(2)}, u32[]{:S(2)}) %all-to-all-start) | async-done | bytes 917536 | tf_op jit(solution)/shard_map/all_to_all | solution.py:59
  44.3 1.3 convolution_convert_fusion.5
  45.6 0.0 all-gather.3.cloned.1.call-update
  45.7 1.8 stack.2
  47.5 10.3 %all-to-all-start.1 = ((bf16[8,448,384]{2,1,0:T(8,128)(2,1)}), bf16[8,448,384]{2,1,0:T(8,128)(2,1)}, u32[]{:S(2)}, u32[]{:S(2)}) async-start(bf16[8,448,384]{2,1,0:T(8,128)(2,1)} %stack.2), calls=%async_computation.1 | async-start | bytes 5505024 | tf_op jit(solution)/shard_map/all_to_all | solution.py:50
  57.8 0.0 reduce-scatter.5.cloned.1.call-start
  57.8 29.3 %all-gather.3.cloned.1.call-done = bf16[768,3584]{1,0:T(8,128)(2,1)} async-done(((bf16[96,3584]{1,0:T(8,128)(2,1)}), bf16[768,3584]{1,0:T(8,128)(2,1)}) %all-gather.3.cloned.1.call-update) | async-done | bytes 5505040 | tf_op jit(solution)/shard_map/all_gather | solution.py:68
  87.2 5.5 %fusion.33 = (bf16[8,48,3584]{2,1,0:T(8,128)(2,1)}, bf16[8,48,3584]{2,1,0:T(8,128)(2,1)}) fusion(bf16[8,96,3584]{2,1,0:T(8,128)(2,1)} %bitcast.71), kind=kLoop, calls=%fused_computation.75 | loop fusion | bytes 11010048 | tf_op jit(solution)/shard_map/slice | solution.py:71
  92.6 30.7 %all-to-all-done.1 = bf16[8,448,384]{2,1,0:T(8,128)(2,1)} async-done(((bf16[8,448,384]{2,1,0:T(8,128)(2,1)}), bf16[8,448,384]{2,1,0:T(8,128)(2,1)}, u32[]{:S(2)}, u32[]{:S(2)}) %all-to-all-start.1) | async-done | bytes 2752544 | tf_op jit(solution)/shard_map/all_to_all | solution.py:50
  123.4 3.0 %fusion.15 = f32[384,128]{1,0:T(8,128)S(1)} fusion(bf16[384,3584]{1,0:T(8,128)(2,1)} %bitcast.61, bf16[3584,384]{1,0:T(8,128)(2,1)} %bitcast.8), kind=kOutput, calls=%fused_computation.32 | convolution fusion | flops 352321536 | bytes 3866624 | tf_op jit(solution)/shard_map/dot_general | solution.py:16
  126.4 2.2 fusion.7
  128.6 2.1 multiply_convert_fusion.2
  130.7 2.1 fusion.13
  132.8 2.1 convolution_convert_fusion
  134.8 2.1 fusion
  136.9 2.8 %pad_maximum_fusion = bf16[8,96,3584]{2,1,0:T(8,128)(2,1)} fusion(bf16[8,48,3584]{2,1,0:T(8,128)(2,1)S(1)} %bitcast.70, bf16[8,48,3584]{2,1,0:T(8,128)(2,1)S(1)} %bitcast.69), kind=kLoop, calls=%fused_computation.3 | loop fusion | flops 11010048 | bytes 11010048 | tf_op jit(solution)/shard_map/concatenate | solution.py:84
  139.7 0.0 reduce-scatter.5.cloned.1.call-update
  139.7 0.0 reduce-scatter.7.cloned.1.call-start
  139.7 2.6 %convolution_convert_fusion.1 = bf16[3584,128]{0,1:T(8,128)(2,1)S(1)} fusion(bf16[384,3584]{1,0:T(8,128)(2,1)} %bitcast.67, bf16[384,128]{1,0:T(8,128)(2,1)S(1)} %get-tuple-element.28), kind=kOutput, calls=%fused_computation.10 | convolution fusion | flops 352780288 | bytes 3768320 | tf_op jit(solution)/shard_map/dot_general | solution.py:16
  142.4 0.7 convolution_convert_fusion.2
  143.1 0.7 convolution_convert_fusion.3
  143.8 1.8 pad_maximum_fusion.1
  145.6 4.6 %copy.27 = bf16[3584,384]{1,0:T(8,128)(2,1)} copy(bf16[3584,384]{0,1:T(8,128)(2,1)} %pad_maximum_fusion.1) | data formatting | bytes 5505024
  150.1 0.0 reduce-scatter.7.cloned.1.call-update
  150.2 22.9 %reduce-scatter.5.cloned.1.call-done = bf16[96,3584]{1,0:T(8,128)(2,1)} async-done(((bf16[768,3584]{1,0:T(8,128)(2,1)}), bf16[96,3584]{1,0:T(8,128)(2,1)}) %reduce-scatter.5.cloned.1.call-update) | async-done | bytes 688144 | tf_op jit(solution)/shard_map/reduce_scatter | solution.py:87
  173.1 2.6 %convolution_convert_fusion.4 = bf16[128,3584]{1,0:T(8,128)(2,1)} fusion(bf16[96,3584]{1,0:T(8,128)(2,1)} %reduce-scatter.5.cloned.1.call-done, s32[96]{0:T(128)S(1)} %broadcast_remainder_fusion, s32[96]{0:T(128)S(1)} %get-tuple-element.42, s32[96]{0:T(128)S(1)} %get-tuple-element.40, s32[96]{0:T(128)S(1)} %get-tuple-element.43, ...), kind=kOutput, calls=%fused_computation.13 | convolution fusion | flops 88612864 | bytes 1607744 | tf_op jit(solution)/shard_map/dot_general | solution.py:16
  175.7 6.9 %all-to-all-start.2 = ((bf16[8,16,3584]{2,1,0:T(8,128)(2,1)}), bf16[8,16,3584]{2,1,0:T(8,128)(2,1)S(1)}, u32[]{:S(2)}, u32[]{:S(2)}) async-start(bf16[8,16,3584]{2,1,0:T(8,128)(2,1)} %bitcast.13), calls=%async_computation.3 | async-start | bytes 1835008 | tf_op jit(solution)/shard_map/all_to_all | solution.py:98
  182.6 44.8 %reduce-scatter.7.cloned.1.call-done = bf16[448,384]{1,0:T(8,128)(2,1)} async-done(((bf16[3584,384]{1,0:T(8,128)(2,1)}), bf16[448,384]{1,0:T(8,128)(2,1)}) %reduce-scatter.7.cloned.1.call-update) | async-done | bytes 344080
  227.4 1.7 fusion.34
  229.2 0.4 bitcast_reduce_fusion
  229.6 0.6 select_reduce_fusion
  230.2 0.4 convolution_bitcast_fusion.1
  230.6 1.4 fusion.2
  232.0 1.3 fusion.3
  (21 shorter events, 0.1 us)
Async XLA Ops:
  7.2 2.8 %copy-start = (bf16[128,3584]{1,0:T(8,128)(2,1)S(1)}, bf16[128,3584]{1,0:T(8,128)(2,1)}, u32[]{:S(2)}) copy-start(bf16[128,3584]{1,0:T(8,128)(2,1)} %param.8) | copy-start | bytes 2752516
  10.3 35.4 %copy-start.4 = (bf16[448,128]{1,0:T(8,128)(2,1)S(1)}, bf16[448,128]{1,0:T(8,128)(2,1)}, u32[]{:S(2)}) copy-start(bf16[448,128]{1,0:T(8,128)(2,1)} %param.13) | copy-start | bytes 344068
  10.3 35.4 %copy-start.5 = (bf16[448,128]{1,0:T(8,128)(2,1)S(1)}, bf16[448,128]{1,0:T(8,128)(2,1)}, u32[]{:S(2)}) copy-start(bf16[448,128]{1,0:T(8,128)(2,1)} %param.12) | copy-start | bytes 344068
  10.3 35.3 %copy-start.6 = (bf16[448,128]{1,0:T(8,128)(2,1)S(1)}, bf16[448,128]{1,0:T(8,128)(2,1)}, u32[]{:S(2)}) copy-start(bf16[448,128]{1,0:T(8,128)(2,1)} %param.11) | copy-start | bytes 344068
  11.3 33.0 %all-to-all-start = ((bf16[8,16,3584]{2,1,0:T(8,128)(2,1)}), bf16[8,16,3584]{2,1,0:T(8,128)(2,1)S(1)}, u32[]{:S(2)}, u32[]{:S(2)}) async-start(bf16[8,16,3584]{2,1,0:T(8,128)(2,1)} %pad_maximum_fusion.2), calls=%async_computation | async-start | bytes 1835008 | tf_op jit(solution)/shard_map/all_to_all | solution.py:59
  18.4 68.8 %all-gather.3.cloned.1.call-start = ((), (), s32[]{:S(2)}) async-start(), calls=%async_computation.6 | async-start | bytes 6193152 | tf_op jit(solution)/shard_map/all_gather | solution.py:68
  47.5 75.9 %all-to-all-start.1 = ((bf16[8,448,384]{2,1,0:T(8,128)(2,1)}), bf16[8,448,384]{2,1,0:T(8,128)(2,1)}, u32[]{:S(2)}, u32[]{:S(2)}) async-start(bf16[8,448,384]{2,1,0:T(8,128)(2,1)} %stack.2), calls=%async_computation.1 | async-start | bytes 5505024 | tf_op jit(solution)/shard_map/all_to_all | solution.py:50
  57.8 115.3 %reduce-scatter.5.cloned.1.call-start = ((), (), s32[]{:S(2)}) async-start(), calls=%async_computation.5 | async-start | bytes 6193152 | tf_op jit(solution)/shard_map/reduce_scatter | solution.py:87
  123.4 3.0 %copy-start.3 = (bf16[8,48,3584]{2,1,0:T(8,128)(2,1)S(1)}, bf16[8,48,3584]{2,1,0:T(8,128)(2,1)}, u32[]{:S(2)}) copy-start(bf16[8,48,3584]{2,1,0:T(8,128)(2,1)} %get-tuple-element.26) | copy-start | bytes 8257540
  126.4 2.2 copy-start.1
  139.7 87.7 %reduce-scatter.7.cloned.1.call-start = ((), (), s32[]{:S(2)}) async-start(), calls=%async_computation.7 | async-start | bytes 3096576
  139.7 2.6 %copy-start.2 = (bf16[8,48,3584]{2,1,0:T(8,128)(2,1)S(1)}, bf16[8,48,3584]{2,1,0:T(8,128)(2,1)}, u32[]{:S(2)}) copy-start(bf16[8,48,3584]{2,1,0:T(8,128)(2,1)} %get-tuple-element.27) | copy-start | bytes 8257540
  150.2 79.4 %copy-start.7 = (s32[128,8]{0,1:T(8,128)S(1)}, s32[128,8]{0,1:T(8,128)}, u32[]{:S(2)}) copy-start(s32[128,8]{0,1:T(8,128)} %param.9) | copy-start | bytes 12292
  175.7 53.5 %all-to-all-start.2 = ((bf16[8,16,3584]{2,1,0:T(8,128)(2,1)}), bf16[8,16,3584]{2,1,0:T(8,128)(2,1)S(1)}, u32[]{:S(2)}, u32[]{:S(2)}) async-start(bf16[8,16,3584]{2,1,0:T(8,128)(2,1)} %bitcast.13), calls=%async_computation.3 | async-start | bytes 1835008 | tf_op jit(solution)/shard_map/all_to_all | solution.py:98
Sparse Core Ops, SparseCore 0:
  45.7 41.3 all-gather.2
  139.8 33.2 reduce-scatter.4
  176.0 51.4 reduce-scatter.6
